TPU v7x, 32 devices: a whole 2x2x4 slice. The times are simulated.
32 devices in a mesh: dp: 8 (over z, y), tensor: 4 (over x, core).
Axes of the slice: x: 2, y: 2, z: 4, core: 2. Of those that a mesh axis runs over, the one named last changes fastest.
Arguments:
- tokens: bfloat16 [16384, 1280], P(('dp', 'tensor')), may hold values from -6 to 6
- cotangent: bfloat16 [16384, 1280], P(('dp', 'tensor')), may hold values from -6 to 6
- block_ids: int32 [8, 2048], P('dp'), may hold values from 0 to 15, never falling along the last dimension, each value on 1 to 256 neighbouring positions
- attn_gain: float32 [1280], replicated, may hold values from 0.5 to 1.5
- w_query: bfloat16 [1280, 1280], P('dp', 'tensor'), may hold values from -0.15625 to 0.15625
- w_key: bfloat16 [1280, 1280], P('dp', 'tensor'), may hold values from -0.15625 to 0.15625
- w_value: bfloat16 [1280, 1280], P('dp', 'tensor'), may hold values from -0.15625 to 0.15625
- query_scale: float32 [80], replicated, may hold values from 0.5 to 2.5
- w_out: bfloat16 [1280, 1280], P('tensor', 'dp'), may hold values from -0.5 to 0.5
- mlp_gain: float32 [1280], replicated, may hold values from 0.5 to 1.5
- w_up: bfloat16 [1280, 1280], P('dp', 'tensor'), may hold values from -0.15625 to 0.15625
- b_up: float32 [1280], replicated, may hold values from -3 to 3
- w_down: bfloat16 [1280, 1280], P('tensor', 'dp'), may hold values from -0.25 to 0.25
- b_down: float32 [1280], replicated, may hold values from -3 to 3
Outputs:
- output: bfloat16 [16384, 1280], P(('dp', 'tensor'))
- d_tokens: bfloat16 [16384, 1280], P(('dp', 'tensor'))
- d_attn_gain: float32 [1280], replicated
- d_w_query: float32 [1280, 1280], P('dp', 'tensor')
- d_w_key: float32 [1280, 1280], P('dp', 'tensor')
- d_w_value: float32 [1280, 1280], P('dp', 'tensor')
- d_query_scale: float32 [80], replicated
- d_w_out: float32 [1280, 1280], P('tensor', 'dp')
- d_mlp_gain: float32 [1280], replicated
- d_w_up: float32 [1280, 1280], P('dp', 'tensor')
- d_b_up: float32 [1280], replicated
- d_w_down: float32 [1280, 1280], P('tensor', 'dp')
- d_b_down: float32 [1280], replicated
Inputs may be any that keep to these rules, and one draw needn't show every extreme that they name: `block_ids`: in each sequence the block numbers never fall along positions, each number from 0 to 15 appears, a block spans 1 to 256 positions, and one block spans exactly 256.
All inputs are finite; a program needn't handle non-finite values.
Results may differ from a plain program's by a relative error of at most 0.014.
The roundings to bfloat16 on the way count: a program that leaves them out, or rounds other values in their place, can miss the bound.
Values may be sent and summed in bfloat16 or wider, within the bound.
A program may use at most 192 MiB of HBM per device.

v0:
```python
import math

import jax
import jax.numpy as jnp
from jax import lax
from jax.experimental import pallas as pl
from jax.experimental.pallas import tpu as pltpu
from jax.sharding import PartitionSpec as P

HD = 80
HP = 128
TILE = 256
BLOCK_MOST = 256
EPSILON = 1e-06
SCORE_BASE = 1.442695041
MASKED = -1e30
BF = jnp.bfloat16
F32 = jnp.float32


def mm(a, b, ca, cb):
    return lax.dot_general(a, b, (((ca,), (cb,)), ((), ())), preferred_element_type=F32)


def reach(tile, length):
    return min((tile + 1) * TILE + BLOCK_MOST, length)


MESH = pl.DeviceIdType.MESH
PARTNERS = (2, 1, 3)
SLOT = {0: 0, 2: 1, 1: 2, 3: 3}


def remote(src, dst, send, recv, where):
    return pltpu.make_async_remote_copy(
        src_ref=src, dst_ref=dst, send_sem=send, recv_sem=recv, device_id=where, device_id_type=MESH
    )


def greet(peers):
    barrier = pltpu.get_barrier_semaphore()
    for where in peers:
        pl.semaphore_signal(barrier, inc=1, device_id=where, device_id_type=MESH)
    pl.semaphore_wait(barrier, len(peers))


def front_kernel(
    dp, far, tok_ref, vec_ref, idr_ref, wq_ref, wk_ref, wv_ref, wo_ref, wu_ref, wd_ref,
    qkv_out, normt_out, wpad_out, att_out, lse_ref, got_out, both_out, wide_out,
    norm, normt, wpad, qkv, att, got, vt_ref, idc_ref, fac, w1_ref, w2_ref, z1, y1, x2, pair,
    sx, rx, sc, rc, sf, rf, sz1, rz1, sy1, ry1, sx2, rx2, sz2, rz2, sy2, ry2, sc2, rc2,
    sx3, rx3, sc3, rc3, st_, rt_, so,
):
    here, me = lax.axis_index("tensor"), lax.axis_index("dp")
    rows, width = tok_ref.shape
    length = norm.shape[0]
    tiles = length // TILE
    heads = qkv.shape[2] // HP
    cols = heads * HD
    depth = width // dp
    packed = depth // 2
    fused = far > 0
    major, minor = me // 2, me % 2

    def at(mask):
        return (me, here ^ mask)

    def xor(mask):
        return here ^ mask

    across = (me ^ 1, here)

    def along(step):
        return (lax.rem(major + step, far) * 2 + minor, here)

    def source(step):
        return lax.rem(major + far - step, far)

    peers = [at(mask) for mask in PARTNERS]
    if fused:
        peers += [across] + [along(step) for step in range(1, far)]
    greet(peers)

    def z_first(w, step):
        return remote(
            w1_ref.at[w], z1.at[step, w], sz1.at[step, w], rz1.at[step, w], along(step)
        )

    def y_first(w, step):
        src = w1_ref.at[w] if isinstance(step, int) and step == 0 else z1.at[step, w]
        return remote(src, y1.at[step, w], sy1.at[step, w], ry1.at[step, w], across)

    swap_two = remote(w2_ref, x2, sx2, rx2, at(2)) if fused else None
    if fused:
        for w, ref in enumerate((wq_ref, wk_ref, wv_ref)):
            w1_ref[w, :, :cols] = ref[:packed, :]
            w1_ref[w, :, cols:] = ref[packed:, :]
            for step in range(1, far):
                z_first(w, step).start()
            y_first(w, 0).start()
        pair[0, :, :cols] = wu_ref[...]
        pair[0, :, cols:] = wd_ref[...]
        pair[1, :, :cols] = wo_ref[...]
        w2_ref[:, :cols] = wo_ref[:packed, :]
        w2_ref[:, cols:] = wo_ref[packed:, :]
        swap_two.start()

    chunk = TILE
    count = rows // chunk

    @pl.loop(0, count)
    def _(c):
        low = pl.multiple_of(c * chunk, chunk)
        v = tok_ref[pl.ds(low, chunk), :].astype(F32)
        hat = v * lax.rsqrt(jnp.mean(v * v, axis=-1, keepdims=True) + EPSILON)
        norm[pl.ds(pl.multiple_of(here * rows + low, chunk), chunk), :] = (
            hat * vec_ref[0:1, :]
        ).astype(BF)

    def rows_of(mask, c):
        return norm.at[pl.ds(pl.multiple_of((here ^ mask) * rows + c * chunk, chunk), chunk), :]

    def send_x(c):
        return remote(rows_of(0, c), rows_of(0, c), sx.at[c], rx.at[c], at(2))

    def send_c(c):
        return remote(rows_of(0, c), rows_of(0, c), sc.at[c], rc.at[c], at(1))

    def forward(c):
        return remote(rows_of(2, c), rows_of(2, c), sf.at[c], rf.at[c], at(1))

    for c in range(count):
        send_x(c).start()
        send_c(c).start()
    idc_ref[...] = jnp.broadcast_to(idr_ref[...].astype(F32), (HP, length)).T.astype(jnp.int32)
    fac[...] = jnp.ones_like(fac)
    fac[0:1, :] = vec_ref[4:5, : heads * HP]

    def project(w, mask, c):
        low = pl.multiple_of(xor(mask) * rows + c * chunk, chunk)
        x = norm[pl.ds(low, chunk), :]
        y = mm(x, wpad[w], 1, 0)
        qkv[w, pl.ds(low, chunk), :] = (y * fac[pl.ds(w, 1), :]).astype(BF)

        @pl.when(w == 2)
        def _():
            normt[:, pl.ds(low, chunk)] = x.astype(F32).T.astype(BF)

    def rows_two(index):
        return pl.ds(pl.multiple_of(index * depth, 16), depth)

    def index_of(step, side):
        return source(step) * 2 + (minor if side == 0 else 1 - minor)

    def block_two(p, index):
        if p == 0:
            return both_out.at[0, rows_two(index), :]
        return wide_out.at[rows_two(index), pl.ds(0, 2 * cols)]

    def held_two(p, step, side):
        return pair.at[p] if step == 0 and side == 0 else block_two(p, index_of(step, side))

    def z_second(p, step):
        return remote(
            pair.at[p], block_two(p, me), sz2.at[p, step], rz2.at[p, step], along(step)
        )

    def y_second(p, step):
        return remote(
            held_two(p, step, 0), block_two(p, index_of(step, 0)),
            sy2.at[p, step], ry2.at[p, step], across,
        )

    def c_second(p, step, side):
        index = index_of(step, side)
        if p == 0:
            dst = both_out.at[2, rows_two(index), :]
        else:
            dst = wide_out.at[rows_two(index), pl.ds(2 * cols, 2 * cols)]
        return remote(
            held_two(p, step, side), dst, sc2.at[p, step, side], rc2.at[p, step, side], at(1)
        )

    def x_second(step, side):
        return remote(
            held_two(0, step, side), both_out.at[1, rows_two(index_of(step, side)), :],
            sx3.at[step, side], rx3.at[step, side], at(2),
        )

    def c_third(step, side):
        spot = rows_two(index_of(step, side))
        return remote(
            both_out.at[1, spot, :], both_out.at[3, spot, :],
            sc3.at[step, side], rc3.at[step, side], at(1),
        )

    def own_two(p):
        return pltpu.make_async_copy(pair.at[p], block_two(p, me), so.at[8 + p])

    def start_second(p):
        for step in range(1, far):
            z_second(p, step).start()
        y_second(p, 0).start()
        own_two(p).start()

    def spread(p, step, side):
        c_second(p, step, side).start()
        if p == 0:
            x_second(step, side).start()

    def after_z(p):
        for step in range(1, far):
            z_second(p, step).wait_recv()
            y_second(p, step).start()
            spread(p, step, 0)

    def after_y(p, step):
        y_second(p, step).wait_recv()
        spread(p, step, 1)

    if fused:
        start_second(0)
        spread(0, 0, 0)
        swap_two.wait_recv()
        for part in range(2):
            pair[1, part * packed : (part + 1) * packed, cols:] = x2[
                :, part * cols : (part + 1) * cols
            ]
        start_second(1)
        spread(1, 0, 0)

    if not fused:
        wpad[...] = wq_ref[...]
        for c in range(count):
            send_c(c).wait_recv()

        @pl.loop(0, 3)
        def _(w):
            @pl.loop(0, 2 * count)
            def _(j):
                project(w, j // count, lax.rem(j, count))

    else:
        wpad[...] = jnp.zeros_like(wpad)

        def unpack(w, block, device):
            for part in range(2):
                low = pl.multiple_of(device * depth + part * packed, 16)
                for h in range(heads):
                    lane = part * cols + h * HD
                    wpad[w, pl.ds(low, packed), h * HP : h * HP + HD] = block[:, lane : lane + HD]

        @pl.loop(0, 3)
        def _(w):
            unpack(w, w1_ref[w], me)

            @pl.loop(1, far)
            def _(step):
                z_first(w, step).wait_recv()
                y_first(w, step).start()
                unpack(w, z1[step, w], source(step) * 2 + minor)

            @pl.loop(0, far)
            def _(step):
                y_first(w, step).wait_recv()
                unpack(w, y1[step, w], source(step) * 2 + 1 - minor)

            @pl.when(w == 0)
            def _():
                for c in range(count):
                    send_c(c).wait_recv()

            @pl.loop(0, 2 * count)
            def _(j):
                project(w, j // count, lax.rem(j, count))

            @pl.when(w == 1)
            def _():
                after_y(0, 0)

        after_z(0)

    @pl.loop(0, count)
    def _(c):
        send_x(c).wait_recv()
        forward(c).start()

        @pl.loop(0, 3)
        def _(w):
            project(w, 2, c)

    @pl.loop(0, count)
    def _(c):
        forward(c).wait_recv()

        @pl.loop(0, 3)
        def _(w):
            project(w, 3, c)

    keep = [
        pltpu.make_async_copy(normt, normt_out, so.at[0]),
        pltpu.make_async_copy(wpad, wpad_out, so.at[1]),
        pltpu.make_async_copy(qkv, qkv_out, so.at[2]),
    ]
    for copy in keep:
        copy.start()

    def trade(h, mask):
        spot = pl.ds(pl.multiple_of((here ^ mask) * rows, HP), rows)
        return remote(
            att.at[h, :, spot], got.at[SLOT[mask], h], st_.at[mask, h], rt_.at[mask, h], at(mask)
        )

    sub = lax.broadcasted_iota(jnp.int32, (HP, length), 0)

    @pl.loop(0, heads)
    def _(h):
        lanes = pl.ds(pl.multiple_of(h * HP, HP), HP)
        vt_ref[...] = jnp.where(sub == HD, 1.0, qkv[2, :, lanes].astype(F32).T).astype(BF)

        def scores(t):
            seen, low = reach(t, length), t * TILE
            st = mm(qkv[1, :seen, lanes], qkv[0, low : low + TILE, lanes], 1, 1)
            visible = idc_ref[low:seen, 0:1] <= idr_ref[:, low : low + TILE]
            masked = jnp.where(visible, st[low:], MASKED)
            return jnp.concatenate([st[:low], masked], 0) if low else masked

        st = scores(0)
        for t in range(tiles):
            later = scores(t + 1) if t + 1 < tiles else None
            seen, low = st.shape[0], t * TILE
            group = jnp.max(st.reshape(seen // 64, 64, TILE), axis=0)
            highest = jnp.max(group, axis=0, keepdims=True)
            weights = jnp.exp(st - highest).astype(BF)
            ot = mm(vt_ref[:, :seen], weights, 1, 0)
            summed = ot[HD : HD + 1, :]
            att[h, :, low : low + TILE] = (ot[:HD] * (1.0 / summed)).astype(BF)
            lse_ref[h, :, low : low + TILE] = highest + jnp.log(summed)
            st = later
        for mask in PARTNERS:
            trade(h, mask).start()
        if fused:
            for n in range(heads):

                @pl.when(h == n)
                def _(n=n):
                    if n == 0:
                        after_y(0, 1)
                    if n == 1:
                        after_y(0, 2)
                        after_y(0, 3)
                    if n == 2:
                        after_z(1)
                        after_y(1, 0)

    got[0] = att[:, :, pl.ds(pl.multiple_of(here * rows, HP), rows)]
    keep.append(pltpu.make_async_copy(att, att_out, so.at[5]))
    keep[-1].start()
    if fused:
        for step in range(far):
            x_second(step, 0).wait_recv()
            c_third(step, 0).start()
        for step in range(1, far):
            after_y(1, step)
        for step in range(far):
            x_second(step, 1).wait_recv()
            c_third(step, 1).start()
    for h in range(heads):
        for mask in PARTNERS:
            trade(h, mask).wait_recv()
    keep.append(pltpu.make_async_copy(got, got_out, so.at[6]))
    keep[-1].start()

    for c in range(count):
        send_x(c).wait_send()
        send_c(c).wait_send()
        forward(c).wait_send()
    for h in range(heads):
        for mask in PARTNERS:
            trade(h, mask).wait_send()
    if fused:
        swap_two.wait_send()
        for w in range(3):
            for step in range(far):
                if step:
                    z_first(w, step).wait_send()
                y_first(w, step).wait_send()
        for p in range(2):
            own_two(p).wait()
            for step in range(far):
                if step:
                    z_second(p, step).wait_send()
                y_second(p, step).wait_send()
                for side in range(2):
                    c_second(p, step, side).wait()
                    if p == 0:
                        x_second(step, side).wait_send()
                        c_third(step, side).wait()
    for copy in keep:
        copy.wait()


def front(dp, far, tokens, vectors, idr, cols, matrices):
    rows, width = tokens.shape
    length = idr.shape[1]
    heads = cols // HD
    wide = heads * HP
    packed = width // dp // 2
    count = rows // TILE
    vmem = pl.BlockSpec(memory_space=pltpu.VMEM)
    hbm = pl.BlockSpec(memory_space=pl.ANY)
    sem = pltpu.SemaphoreType.DMA
    far_n = max(far, 1)
    fused = far > 0
    small = (packed, 2 * cols) if fused else (16, 128)
    return pl.pallas_call(
        lambda *refs: front_kernel(dp, far, *refs),
        out_shape=[
            jax.ShapeDtypeStruct((3, length, wide), BF),
            jax.ShapeDtypeStruct((width, length), BF),
            jax.ShapeDtypeStruct((3, width, wide), BF),
            jax.ShapeDtypeStruct((heads, HD, length), BF),
            jax.ShapeDtypeStruct((heads, 1, length), F32),
            jax.ShapeDtypeStruct((4, heads, HD, rows), BF),
            jax.ShapeDtypeStruct((4, width, 2 * cols) if fused else (16, 128), BF),
            jax.ShapeDtypeStruct((width, 4 * cols) if fused else (16, 128), BF),
        ],
        in_specs=[vmem] * 9,
        out_specs=[hbm] * 4 + [vmem] + [hbm] * 3,
        scratch_shapes=[
            pltpu.VMEM((length, width), BF),
            pltpu.VMEM((width, length), BF),
            pltpu.VMEM((3, width, wide), BF),
            pltpu.VMEM((3, length, wide), BF),
            pltpu.VMEM((heads, HD, length), BF),
            pltpu.VMEM((4, heads, HD, rows), BF),
            pltpu.VMEM((HP, length), BF),
            pltpu.VMEM((length, HP), jnp.int32),
            pltpu.VMEM((8, wide), F32),
            pltpu.VMEM((3,) + small, BF),
            pltpu.VMEM(small, BF),
            pltpu.VMEM((far_n, 3) + small, BF),
            pltpu.VMEM((far_n, 3) + small, BF),
            pltpu.VMEM(small, BF),
            pltpu.VMEM((2, 2 * packed, 2 * cols) if fused else (2, 16, 128), BF),
            sem((count,)), sem((count,)), sem((count,)), sem((count,)), sem((count,)), sem((count,)),
            sem((far_n, 3)), sem((far_n, 3)), sem((far_n, 3)), sem((far_n, 3)),
            sem, sem,
            sem((2, far_n)), sem((2, far_n)), sem((2, far_n)), sem((2, far_n)),
            sem((2, far_n, 2)), sem((2, far_n, 2)),
            sem((far_n, 2)), sem((far_n, 2)), sem((far_n, 2)), sem((far_n, 2)),
            sem((4, heads)), sem((4, heads)),
            sem((12,)),
        ],
        compiler_params=pltpu.CompilerParams(
            vmem_limit_bytes=60 << 20, collective_id=1, has_side_effects=True
        ),
    )(tokens, vectors, idr, *matrices)


def mid_kernel(
    tok_ref, cot_ref, got_ref, vec_ref, wide_ref, both_ref,
    out_ref, dhid_ref, drec_out, xk_out, xg_out, pb_out, early_ref,
    w, both, att, n2, act, dpre, branch, hid, give, grec, db, drec, kept, bs,
    ss, rs, sg, rg, so,
):
    here, me = lax.axis_index("tensor"), lax.axis_index("dp")
    rows, width = tok_ref.shape
    wide = w.shape[1]
    cols = wide // 4
    pair = 2 * cols
    chunk = TILE
    half = chunk // 2
    count = rows // chunk

    def at(mask):
        return (me, here ^ mask)

    loads = [
        pltpu.make_async_copy(both_ref, both, so.at[1]),
        pltpu.make_async_copy(wide_ref, w.at[0], so.at[0]),
    ]
    for copy in loads:
        copy.start()
    greet([at(mask) for mask in PARTNERS])
    att[...] = got_ref[...].astype(F32).T.astype(BF)
    early_ref[...] = jnp.zeros_like(early_ref)
    bs[...] = jnp.zeros_like(bs)
    loads[0].wait()

    @pl.loop(0, width // chunk)
    def _(j):
        spot = pl.ds(pl.multiple_of(j * chunk, chunk), chunk)
        for i in range(4):
            w[1, spot, i * cols : (i + 1) * cols] = both[i, spot, :cols]
            w[2, spot, i * cols : (i + 1) * cols] = both[i, spot, cols:]

    loads[1].wait()

    def trade(c, mask):
        return remote(
            db.at[c, SLOT[mask]], drec.at[c, SLOT[mask]],
            ss.at[c, mask], rs.at[c, mask], at(mask),
        )

    @pl.loop(0, count)
    def _(c):
        low = pl.multiple_of(c * chunk, chunk)
        spot = pl.ds(low, chunk)
        hidden = tok_ref[spot, :].astype(F32) + mm(att[spot, :], w[0], 1, 1)
        hid[spot, :] = hidden
        cot = cot_ref[spot, :]
        d_act = mm(cot, w[2], 1, 0)
        inverse = lax.rsqrt(jnp.mean(hidden * hidden, axis=-1, keepdims=True) + EPSILON)
        hat = hidden * inverse
        normed = (hat * vec_ref[1:2, :]).astype(BF)
        n2[spot, :] = normed
        pre = mm(normed, w[1], 1, 0) + vec_ref[2:3, :]
        sig = jax.nn.sigmoid(pre)
        act[spot, :] = (pre * sig).astype(BF)
        d_pre = (d_act * sig * (1.0 + pre * (1.0 - sig))).astype(BF)
        dpre[spot, :] = d_pre
        d_n2 = mm(d_pre, w[1], 1, 1)
        scaled = d_n2 * vec_ref[1:2, :]
        cot_f32 = cot.astype(F32)
        d_hidden = cot_f32 + inverse * (
            scaled - hat * jnp.mean(scaled * hat, axis=-1, keepdims=True)
        )
        dhid_ref[spot, :] = d_hidden
        br = d_hidden.astype(BF)
        branch[spot, :] = br
        d_att = mm(br, w[0], 1, 0).astype(BF)
        for i in range(4):
            for part in range(2):
                db[c, i, :, part * cols : (part + 1) * cols] = d_att[
                    part * half : (part + 1) * half, i * cols : (i + 1) * cols
                ]
        for mask in PARTNERS:
            trade(c, mask).start()
        drec[c, 0] = db[c, 0]
        early_ref[0:1, :] += jnp.sum(d_n2 * hat, axis=0, keepdims=True)
        early_ref[1:2, :] += jnp.sum(cot_f32, axis=0, keepdims=True)
        bs[0:1, :] += jnp.sum(d_pre.astype(F32), axis=0, keepdims=True)

    pieces = ((branch, att), (n2, dpre), (cot_ref, act))

    def hand(i):
        return remote(give.at[i], grec.at[i], sg.at[i], rg.at[i], at(1))

    for i in range(3):

        @pl.loop(0, width // chunk)
        def _(j):
            spot = pl.ds(pl.multiple_of(j * chunk, chunk), chunk)
            left, right = pieces[i]
            g = mm(left[:, spot], right[...], 0, 0).astype(BF)
            give[i, spot, :] = g[:, pair:]
            if i == 0:
                kept[2, spot, :] = g[:, :pair]
            else:
                lane = (i - 1) * cols
                kept[0, spot, lane : lane + cols] = g[:, :cols]
                kept[1, spot, lane : lane + cols] = g[:, cols:pair]

        hand(i).start()

    for i in range(4):
        place = here ^ (0, 2, 1, 3)[i]
        early_ref[pl.ds(2 + place, 1), 0:cols] = bs[0:1, i * cols : (i + 1) * cols]

    @pl.loop(0, count)
    def _(c):
        spot = pl.ds(pl.multiple_of(c * chunk, chunk), chunk)
        out_ref[spot, :] = (hid[spot, :] + mm(act[spot, :], w[2], 1, 1) + vec_ref[3:4, :]).astype(BF)

    for i in range(3):
        hand(i).wait_recv()

        @pl.loop(0, width // chunk)
        def _(j):
            spot = pl.ds(pl.multiple_of(j * chunk, chunk), chunk)
            came = grec[i, spot, :]
            if i == 0:
                kept[2, spot, :] += came
            else:
                lane = (i - 1) * cols
                kept[0, spot, lane : lane + cols] += came[:, :cols]
                kept[1, spot, lane : lane + cols] += came[:, cols:]

        if i == 0:
            keep = [pltpu.make_async_copy(kept.at[2], pb_out, so.at[3])]
            keep[0].start()
    keep.append(pltpu.make_async_copy(kept.at[0], xk_out, so.at[4]))
    keep.append(pltpu.make_async_copy(kept.at[1], xg_out, so.at[5]))
    for copy in keep[1:]:
        copy.start()
    for c in range(count):
        for mask in PARTNERS:
            trade(c, mask).wait_recv()
    keep.append(pltpu.make_async_copy(drec, drec_out, so.at[6]))
    keep[-1].start()
    for c in range(count):
        for mask in PARTNERS:
            trade(c, mask).wait_send()
    for i in range(3):
        hand(i).wait_send()
    for copy in keep:
        copy.wait()


def middle(tokens, cotangent, got, vectors, wide, both):
    rows, width = tokens.shape
    all_cols = wide.shape[1]
    cols = all_cols // 4
    count = rows // TILE
    vmem = pl.BlockSpec(memory_space=pltpu.VMEM)
    hbm = pl.BlockSpec(memory_space=pl.ANY)
    sem = pltpu.SemaphoreType.DMA
    blocks = (count, 4, TILE // 2, 2 * cols)
    halves = jax.ShapeDtypeStruct((width, 2 * cols), BF)
    return pl.pallas_call(
        mid_kernel,
        out_shape=[
            jax.ShapeDtypeStruct((rows, width), BF),
            jax.ShapeDtypeStruct((rows, width), F32),
            jax.ShapeDtypeStruct(blocks, BF),
            halves,
            halves,
            halves,
            jax.ShapeDtypeStruct((16, width), F32),
        ],
        in_specs=[vmem] * 4 + [hbm] * 2,
        out_specs=[vmem, vmem, hbm, hbm, hbm, hbm, vmem],
        scratch_shapes=[
            pltpu.VMEM((3, width, all_cols), BF),
            pltpu.VMEM((4, width, 2 * cols), BF),
            pltpu.VMEM((rows, all_cols), BF),
            pltpu.VMEM((rows, width), BF),
            pltpu.VMEM((rows, all_cols), BF),
            pltpu.VMEM((rows, all_cols), BF),
            pltpu.VMEM((rows, width), BF),
            pltpu.VMEM((rows, width), F32),
            pltpu.VMEM((3, width, 2 * cols), BF),
            pltpu.VMEM((3, width, 2 * cols), BF),
            pltpu.VMEM(blocks, BF),
            pltpu.VMEM(blocks, BF),
            pltpu.VMEM((3, width, 2 * cols), BF),
            pltpu.VMEM((8, all_cols), F32),
            sem((count, 4)), sem((count, 4)), sem((3,)), sem((3,)), sem((8,)),
        ],
        compiler_params=pltpu.CompilerParams(
            vmem_limit_bytes=60 << 20, collective_id=2, has_side_effects=True
        ),
    )(tokens, cotangent, got, vectors, wide, both)


def back_kernel(
    dp, far, o_ref, lse_ref, drec_ref, vec_ref, idr_ref, xk_ref, early_ref,
    qkv_hbm, xg_ref, pb_ref, tok_hbm, dhid_hbm, normt_hbm, wpad_hbm,
    dtok_ref, dq_out, dk_out, dv_out, dout_ref, dup_ref, ddown_ref, sums_ref,
    do, dka, dva, kt_ref, idc_ref, dqkv, tok, dhid, normt, wpad,
    xrec, pbown, yrec, zrec, last, lastsend, lastrec,
    gpay, gyrec, gzrec, ownsum, near, fo, crec, fs, frec, nrec, qsum, lvec, ar, arec, aorder,
    so, sxa, rxa, sy, ry, sz, rz, sl, rl, sgy, rgy, sgz, rgz, sfo, rfo, sfs, rfs, sno, rno, sar, rar,
):
    here, me = lax.axis_index("tensor"), lax.axis_index("dp")
    heads, _, length = o_ref.shape
    rows, width = tok.shape
    cols = heads * HD
    tiles = length // TILE
    depth = width // dp
    packed = depth // 2
    fused = far > 0
    major, minor = me // 2, me % 2
    chunk = TILE
    count = rows // chunk

    def at(mask):
        return (me, here ^ mask)

    across = (me ^ 1, here)

    def along(step):
        return (lax.rem(major + step, far) * 2 + minor, here)

    def target(step):
        return lax.rem(major + step, far)

    loads = [
        pltpu.make_async_copy(src, dst, so.at[i])
        for i, (src, dst) in enumerate(
            ((wpad_hbm, wpad), (normt_hbm, normt), (tok_hbm, tok), (dhid_hbm, dhid))
        )
    ]
    load_qkv = pltpu.make_async_copy(qkv_hbm, dqkv, so.at[4])
    load_qkv.start()
    if fused:
        load_pb = pltpu.make_async_copy(pb_ref.at[:, minor], pbown, so.at[5])
        load_pb.start()
    for copy in loads:
        copy.start()
    peers = [at(2), at(1)]
    if fused:
        peers += [across] + [along(step) for step in range(1, far)]
    greet(peers)

    turn = list(range(1, far)) + [0]

    def x_send(step):
        spot = target(step)
        return remote(xg_ref.at[spot], xrec.at[spot], sxa.at[step], rxa.at[step], at(2))

    def y_send(p, step):
        spot = target(step)
        src = xrec.at[spot, 1 - minor] if p == 0 else pb_ref.at[spot, 1 - minor]
        return remote(src, yrec.at[p, spot], sy.at[p, step], ry.at[p, step], across)

    def z_send(p, step):
        return remote(
            yrec.at[p, target(step)], zrec.at[p, step - 1],
            sz.at[p, step], rz.at[p, step], along(step),
        )

    def after_x(step):
        x_send(step).wait_recv()
        spot = target(step)
        xrec[spot] = xk_ref[spot] + xrec[spot]
        y_send(0, step).start()

    def after_y(p, step):
        y_send(p, step).wait_recv()
        spot = target(step)
        mine = xrec[spot, minor] if p == 0 else pbown[spot]

        @pl.when(step != 0)
        def _():
            yrec[p, spot] = mine + yrec[p, spot]
            z_send(p, step).start()

        @pl.when(step == 0)
        def _():
            last[p] = mine.astype(F32) + yrec[p, spot].astype(F32)

    def after_z(p):
        for step in range(1, far):
            z_send(p, step).wait_recv()
            last[p] += zrec[p, step - 1].astype(F32)

    if fused:
        for step in turn:
            x_send(step).start()
            y_send(1, step).start()

    do[...] = jnp.zeros_like(do)
    half = chunk // 2
    for c in range(count):
        for i, mask in enumerate((0, 2, 1, 3)):
            block = drec_ref[c, i]
            for part in range(2):
                low = pl.multiple_of((here ^ mask) * rows + c * chunk + part * half, half)
                for h in range(heads):
                    lane = part * cols + h * HD
                    do[h, pl.ds(low, half), 0:HD] = block[:, lane : lane + HD]
    qsum[...] = jnp.zeros_like(qsum)
    if fused:
        gpay[...] = jnp.zeros_like(gpay)
    idc_ref[...] = jnp.broadcast_to(idr_ref[...].astype(F32), (HP, length)).T.astype(jnp.int32)

    load_qkv.wait()
    if fused:
        load_pb.wait()

    def one_head(h):
        lanes = pl.ds(pl.multiple_of(h * HP, HP), HP)
        kt_ref[...] = dqkv[1, :, lanes].astype(F32).T.astype(BF)
        dka[...] = jnp.zeros_like(dka)
        dva[...] = jnp.zeros_like(dva)
        scale_sum = jnp.zeros((1, HP), F32)
        for t in range(tiles):
            seen, low = reach(t, length), t * TILE
            spot = slice(low, low + TILE)
            qt = dqkv[0, spot, lanes]
            dot_ = do[h, spot, :]
            delta = jnp.sum(
                dot_.astype(F32).T[:HD] * o_ref[h, :, spot].astype(F32), axis=0, keepdims=True
            )
            st = mm(dqkv[1, :seen, lanes], qt, 1, 1)
            p = jnp.exp(st - lse_ref[h, :, spot])
            visible = idc_ref[low:seen, 0:1] <= idr_ref[:, spot]
            pm = jnp.where(visible, p[low:], 0.0)
            p = jnp.concatenate([p[:low], pm], 0) if low else pm
            d_p = mm(dqkv[2, :seen, lanes], dot_, 1, 1)
            ds = (p * (d_p - delta)).astype(BF)
            dva[:seen, :] += mm(p.astype(BF), dot_, 1, 0)
            dka[:seen, :] += mm(ds, qt, 1, 0)
            dq = mm(kt_ref[:, :seen], ds, 1, 0).T
            scale_sum = scale_sum + jnp.sum(dq * qt.astype(F32), axis=0, keepdims=True)
            dqkv[0, spot, lanes] = (dq * vec_ref[4:5, :HP]).astype(BF)
        dqkv[1, :, lanes] = dka[...].astype(BF)
        dqkv[2, :, lanes] = dva[...].astype(BF)
        qsum[0:1, :] += scale_sum

    group = 2 * HD

    def weight_blocks(n, step):
        spot = target(step)
        low = pl.multiple_of(spot * 2 * depth, 16)
        lanes = slice(n * 2 * HP, (n + 1) * 2 * HP)
        dots = jnp.zeros((2 * depth, 1), F32)
        for i in range(3):
            g = mm(normt[pl.ds(low, 2 * depth), :], dqkv[i, :, lanes], 1, 0)
            dots = dots + jnp.sum(
                g * wpad[i, pl.ds(low, 2 * depth), lanes].astype(F32), axis=1, keepdims=True
            )
            g = g.astype(BF)
            for side in range(2):
                for h in range(2):
                    lane = i * group + h * HD
                    gpay[n, spot, side, :, lane : lane + HD] = g[
                        side * depth : (side + 1) * depth, h * HP : h * HP + HD
                    ]
        flat = jnp.broadcast_to(dots, (2 * depth, HP)).T[0:1, :]
        lvec[n, pl.ds(spot * 2, 1), :] = flat[:, :depth]
        lvec[n, pl.ds(spot * 2 + 1, 1), :] = flat[:, depth:]

    def gy_send(n, step):
        spot = target(step)
        return remote(
            gpay.at[n, spot, 1 - minor], gyrec.at[n, spot], sgy.at[n, step], rgy.at[n, step], across
        )

    def gz_send(n, step):
        return remote(
            gyrec.at[n, target(step)], gzrec.at[n, step - 1],
            sgz.at[n, step], rgz.at[n, step], along(step),
        )

    def weight_pair(n):
        @pl.loop(0, far)
        def _(j):
            step = lax.rem(j + 1, far)
            weight_blocks(n, step)
            gy_send(n, step).start()

    def gz_start(n, step):
        gy_send(n, step).wait_recv()
        spot = target(step)
        mine = gpay[n, spot, minor]

        @pl.when(step != 0)
        def _():
            gyrec[n, spot] = mine + gyrec[n, spot]
            gz_send(n, step).start()

        @pl.when(step == 0)
        def _():
            ownsum[n] = mine.astype(F32) + gyrec[n, spot].astype(F32)

    @pl.loop(0, heads)
    def _(h):
        one_head(h)
        if fused:
            after_x(lax.rem(h + 1, far))

            @pl.when(h < 2)
            def _():
                @pl.loop(0, 2)
                def _(k):
                    after_y(1, lax.rem(2 * h + k + 1, far))

            @pl.when(h > 0)
            def _():
                after_y(0, h)

            @pl.when(h == 1)
            def _():
                for copy in loads[:2]:
                    copy.wait()
                weight_pair(0)

            @pl.when(h == 2)
            def _():
                @pl.loop(0, far)
                def _(j):
                    gz_start(0, lax.rem(j + 1, far))

    if not fused:
        for copy in loads[:2]:
            copy.wait()

    def part(mask, c):
        spot = pl.ds(pl.multiple_of((here ^ mask) * rows + c * chunk, chunk), chunk)
        total = mm(dqkv[0, spot, :], wpad[0], 1, 1)
        total = total + mm(dqkv[1, spot, :], wpad[1], 1, 1)
        return total + mm(dqkv[2, spot, :], wpad[2], 1, 1)

    def c_far(c):
        return remote(fo.at[c], crec.at[c], sfo.at[c], rfo.at[c], at(1))

    def x_far(c):
        return remote(fs.at[c], frec.at[c], sfs.at[c], rfs.at[c], at(2))

    def c_near(c):
        return remote(fo.at[c], nrec.at[c], sno.at[c], rno.at[c], at(1))

    def far_chunk(c):
        fo[c] = part(3, c).astype(BF)
        c_far(c).start()

    def far_sum(c):
        own = part(2, c)
        c_far(c).wait_recv()
        fs[c] = (own + crec[c].astype(F32)).astype(BF)

    def hop(n, where):
        return remote(ar.at[n], arec.at[n], sar.at[n], rar.at[n], where)

    def z_hop(step):
        return remote(ar.at[3], arec.at[3 + step], sar.at[3 + step], rar.at[3 + step], along(step))

    if fused:
        far_chunk(0)
        far_sum(0)
        x_far(0).start()
        after_y(0, turn[far - 1])
        weight_pair(1)
        ar[0] = jnp.zeros_like(ar[0])
        ar[0, 0:6, :] = early_ref[0:6, :]
        ar[0, 6:7, 0:HP] = qsum[0:1, :]
        ar[0, 8:16, 0:depth] = lvec[0] + lvec[1]
        hop(0, at(1)).start()
        for c in range(1, count):
            far_chunk(c)

        @pl.loop(1, 3)
        def _(step):
            gz_start(1, step)

        hop(0, at(1)).wait_recv()
        ar[1] = ar[0] + arec[0]
        hop(1, at(2)).start()
        for c in range(1, count):
            far_sum(c)
            x_far(c).start()
        after_z(1)
        for piece in range(2):
            last_half = last[1, piece * packed : (piece + 1) * packed, cols:]
            lastsend[:, piece * cols : (piece + 1) * cols] = last_half.astype(BF)
        cross = remote(lastsend, lastrec, sl, rl, at(2))
        cross.start()
    else:
        for c in range(count):
            far_chunk(c)
            far_sum(c)
            x_far(c).start()

        @pl.loop(0, 3)
        def _(i):
            for j in range(width // chunk):
                dq_out[i, j * chunk : (j + 1) * chunk, :] = mm(
                    normt[j * chunk : (j + 1) * chunk, :], dqkv[i], 1, 0
                )

    if not fused:
        sums_ref[...] = jnp.zeros_like(sums_ref)
        sums_ref[0:6, :] = early_ref[0:6, :]
        sums_ref[6:7, 0:HP] = qsum[0:1, :]

    @pl.loop(0, count)
    def _(c):
        c_far(c).wait_send()
        fo[c] = part(1, c).astype(BF)
        c_near(c).start()

    if fused:

        @pl.loop(0, 2)
        def _(j):
            gz_start(1, lax.rem(j + 3, far))

        hop(1, at(2)).wait_recv()
        ar[2] = ar[1] + arec[1]
        hop(2, across).start()
        after_z(0)
        dup_ref[...] = last[0, :, :cols]
        ddown_ref[...] = last[0, :, cols:]
    for copy in loads[2:]:
        copy.wait()

    @pl.loop(0, count)
    def _(c):
        near[c] = part(0, c)

    if fused:
        hop(2, across).wait_recv()
        ar[3] = ar[2] + arec[2]
        for step in range(1, far):
            z_hop(step).start()
        cross.wait_recv()
        arrived = jnp.concatenate([lastrec[:, :cols], lastrec[:, cols:]], axis=0)
        dout_ref[...] = last[1, :, :cols] + arrived.astype(F32)

    @pl.loop(0, count)
    def _(c):
        c_near(c).wait_recv()
        x_far(c).wait_recv()
        d_normed = near[c] + nrec[c].astype(F32) + frec[c].astype(F32)
        spot = pl.ds(pl.multiple_of(c * chunk, chunk), chunk)
        v = tok[spot, :].astype(F32)
        inverse = lax.rsqrt(jnp.mean(v * v, axis=-1, keepdims=True) + EPSILON)
        hat = v * inverse
        scaled = d_normed * vec_ref[0:1, :]
        dtok_ref[spot, :] = (
            dhid[spot, :]
            + inverse * (scaled - hat * jnp.mean(scaled * hat, axis=-1, keepdims=True))
        ).astype(BF)

    if fused:
        for n in range(2):
            for step in range(1, far):
                gz_send(n, step).wait_recv()
                ownsum[n] += gzrec[n, step - 1].astype(F32)
            for i, ref in enumerate((dq_out, dk_out, dv_out)):
                ref[:, n * group : (n + 1) * group] = ownsum[n, :, i * group : (i + 1) * group]
        aorder[major] = ar[3]
        for step in range(1, far):
            z_hop(step).wait_recv()
            aorder[lax.rem(major + far - step, far)] = arec[3 + step]
        sums_ref[...] = (aorder[0] + aorder[1]) + (aorder[2] + aorder[3])
    else:
        dk_out[...] = jnp.zeros_like(dk_out)
        dv_out[...] = jnp.zeros_like(dv_out)
        dout_ref[...] = jnp.zeros_like(dout_ref)
        dup_ref[...] = jnp.zeros_like(dup_ref)
        ddown_ref[...] = jnp.zeros_like(ddown_ref)

    for c in range(count):
        x_far(c).wait_send()
        c_near(c).wait_send()
    if fused:
        for step in range(far):
            x_send(step).wait_send()
            for p in range(2):
                gy_send(p, step).wait_send()
                y_send(p, step).wait_send()
            if step:
                gz_send(0, step).wait_send()
                gz_send(1, step).wait_send()
                z_hop(step).wait_send()
                for p in range(2):
                    z_send(p, step).wait_send()
        cross.wait_send()
        hop(0, at(1)).wait_send()
        hop(1, at(2)).wait_send()
        hop(2, across).wait_send()


def backward(dp, far, o, lse, drec, vectors, idr, xk, early, qkv, xg, pb,
             tokens, d_hidden, normt, wpad):
    heads, _, length = o.shape
    rows, width = tokens.shape
    cols, wide = heads * HD, heads * HP
    depth = width // dp
    packed = depth // 2
    count = rows // TILE
    fused = far > 0
    far_n = max(far, 1)
    vmem = pl.BlockSpec(memory_space=pltpu.VMEM)
    hbm = pl.BlockSpec(memory_space=pl.ANY)
    sem = pltpu.SemaphoreType.DMA
    tiny = jax.ShapeDtypeStruct((8, 128), F32)
    shard = jax.ShapeDtypeStruct((depth, cols), F32) if fused else tiny
    whole = shard if fused else jax.ShapeDtypeStruct((3, width, wide), F32)

    def buf(*shape, dtype=BF, only=True):
        return pltpu.VMEM(shape if fused or not only else (8, 128), dtype)

    pair = 2 * cols
    return pl.pallas_call(
        lambda *refs: back_kernel(dp, far, *refs),
        out_shape=[jax.ShapeDtypeStruct((rows, width), BF), whole, shard, shard, shard, shard,
                   shard, jax.ShapeDtypeStruct((16, width), F32)],
        in_specs=[vmem] * 7 + [hbm] * 7,
        out_specs=[vmem] * 8,
        scratch_shapes=[
            buf(heads, length, HP, only=False),
            buf(length, HP, dtype=F32, only=False),
            buf(length, HP, dtype=F32, only=False),
            buf(HP, length, only=False),
            buf(length, HP, dtype=jnp.int32, only=False),
            buf(3, length, wide, only=False),
            buf(rows, width, only=False),
            buf(rows, width, dtype=F32, only=False),
            buf(width, length, only=False),
            buf(3, width, wide, only=False),
            buf(far_n, 2, depth, pair),
            buf(far_n, depth, pair),
            buf(2, far_n, depth, pair),
            buf(2, far_n - 1, depth, pair),
            buf(2, depth, pair, dtype=F32),
            buf(packed, pair),
            buf(packed, pair),
            buf(2, far_n, 2, depth, 4 * HP),
            buf(2, far_n, depth, 4 * HP),
            buf(2, far_n - 1, depth, 4 * HP),
            buf(2, depth, 4 * HP, dtype=F32),
            buf(count, TILE, width, dtype=F32, only=False),
            buf(count, TILE, width, only=False),
            buf(count, TILE, width, only=False),
            buf(count, TILE, width, only=False),
            buf(count, TILE, width, only=False),
            buf(count, TILE, width, only=False),
            buf(8, HP, dtype=F32, only=False),
            buf(2, dp, depth, dtype=F32),
            buf(4, 16, width, dtype=F32),
            buf(3 + far_n, 16, width, dtype=F32),
            buf(far_n, 16, width, dtype=F32),
            sem((6,)),
            sem((far_n,)), sem((far_n,)),
            sem((2, far_n)), sem((2, far_n)), sem((2, far_n)), sem((2, far_n)),
            sem, sem,
            sem((2, far_n)), sem((2, far_n)), sem((2, far_n)), sem((2, far_n)),
            sem((count,)), sem((count,)), sem((count,)), sem((count,)), sem((count,)), sem((count,)),
            sem((3 + far_n,)), sem((3 + far_n,)),
        ],
        compiler_params=pltpu.CompilerParams(
            vmem_limit_bytes=62 << 20, collective_id=3, has_side_effects=True
        ),
    )(o, lse, drec, vectors, idr, xk, early, qkv, xg, pb,
      tokens, d_hidden, normt, wpad)


def finish_kernel(dp, cols, scale_ref, sums_ref, vec_ref, *refs):
    moves, outs, held = refs[:8], refs[8:21], refs[21:29]
    row, sem = refs[29:]
    width = vec_ref.shape[1]
    depth = width // dp
    places = (0, 1, 3, 4, 5, 7, 9, 11)
    enter = [pltpu.make_async_copy(moves[i], held[i], sem.at[i]) for i in range(8)]
    leave = [pltpu.make_async_copy(held[i], outs[places[i]], sem.at[8 + i]) for i in range(8)]
    for copy in enter:
        copy.start()
    outs[6][...] = sums_ref[6, 0:HP] * scale_ref[0, :]
    outs[8][...] = sums_ref[0, :]
    outs[12][...] = sums_ref[1, :]
    row[...] = jnp.zeros_like(row)
    for i in range(width // cols):
        row[0:1, i * cols : (i + 1) * cols] = sums_ref[2 + i : 3 + i, :cols]
    for i in range(dp):
        spot = slice(i * depth, (i + 1) * depth)
        row[1:2, spot] = sums_ref[8 + i : 9 + i, :depth] / vec_ref[0:1, spot]
    outs[10][...] = row[0, :]
    outs[2][...] = row[1, :]
    for come, go in zip(enter, leave):
        come.wait()
        go.start()
    for copy in leave:
        copy.wait()


def finish(dp, cols, scale, sums, vectors, moves):
    width = vectors.shape[1]
    vmem = pl.BlockSpec(memory_space=pltpu.VMEM)
    hbm = pl.BlockSpec(memory_space=pl.ANY)
    row = jax.ShapeDtypeStruct((width,), F32)
    like = [jax.ShapeDtypeStruct(v.shape, v.dtype) for v in moves]
    shapes = like[:2] + [row] + like[2:5] + [jax.ShapeDtypeStruct((HP,), F32)]
    shapes += [like[5], row, like[6], row, like[7], row]
    small = (2, 6, 8, 10, 12)
    return pl.pallas_call(
        lambda *refs: finish_kernel(dp, cols, *refs),
        out_shape=shapes,
        in_specs=[vmem] * 3 + [hbm] * 8,
        out_specs=[vmem if i in small else hbm for i in range(13)],
        scratch_shapes=[pltpu.VMEM(v.shape, v.dtype) for v in moves]
        + [pltpu.VMEM((8, width), F32), pltpu.SemaphoreType.DMA((16,))],
        compiler_params=pltpu.CompilerParams(vmem_limit_bytes=60 << 20),
    )(scale, sums, vectors, *moves)


def swap(v, axis, size, mask):
    return lax.ppermute(v, axis, [(i, i ^ mask) for i in range(size)])


def gather_dp(shard):
    return lax.all_gather(shard, "dp", axis=0, tiled=True)


def scatter_dp(grad, size):
    return lax.psum_scatter(grad, "dp", scatter_dimension=0, tiled=True)


def pad_heads(w):
    rows, cols = w.shape
    w = w.reshape(rows, cols // HD, HD)
    return jnp.pad(w, ((0, 0), (0, 0), (0, HP - HD))).reshape(rows, cols // HD * HP)


def trim_heads(w):
    rows, cols = w.shape
    return w.reshape(rows, cols // HP, HP)[:, :, :HD].reshape(rows, cols // HP * HD)


def body(dp, tensor, tokens, cotangent, block_ids, attn_gain, w_query, w_key, w_value,
         query_scale, w_out, mlp_gain, w_up, b_up, w_down, b_down):
    assert tensor == 4
    here = lax.axis_index("tensor")
    rows, width = tokens.shape
    length = rows * tensor
    cols = w_query.shape[1]
    heads = cols // HD
    order = [here, here ^ 2, here ^ 1, here ^ 3]

    softplus = jnp.log1p(jnp.exp(query_scale))
    factor = jnp.pad(SCORE_BASE / math.sqrt(HD) * softplus, (0, HP - HD))
    b_rel = jnp.concatenate([lax.dynamic_slice(b_up, (at * cols,), (cols,)) for at in order])
    repeat = jnp.pad(jnp.tile(factor, heads), (0, width - heads * HP))
    vectors = jnp.concatenate([attn_gain, mlp_gain, b_rel, b_down, repeat]).reshape(5, width)

    far = dp // 2 if dp == 8 else 0
    matrices = (w_query, w_key, w_value, w_out.T, w_up, w_down.T)
    if not far:
        pair = [jnp.concatenate([w, swap(w, "tensor", tensor, 2)], axis=1) for w in matrices[3:]]
        half = gather_dp(jnp.concatenate(pair, axis=1)).reshape(width, 3, 2 * cols)
        both = jnp.concatenate([half, swap(half, "tensor", tensor, 1)], axis=2)
        full = gather_dp(jnp.concatenate(matrices[:3], axis=1))
        first = jnp.stack([pad_heads(full[:, i * cols : (i + 1) * cols]) for i in range(3)])
        matrices = (first,) + matrices[1:]
    qkv, normed_t, padded, attended, lse, got, pairs, wide = front(
        dp, far, tokens, vectors, block_ids, cols, matrices
    )
    if not far:
        wide = both[:, 0]
        pairs = both[:, 1:].reshape(width, 2, 4, cols).transpose(2, 0, 1, 3)
        pairs = pairs.reshape(4, width, 2 * cols)

    output, d_hidden, received, xk, xg, pb, early = middle(
        tokens, cotangent, got.reshape(4 * cols, rows), vectors, wide, pairs
    )
    depth = width // dp
    if far:
        xk, xg, pb = (v.reshape(far, 2, depth, 2 * cols) for v in (xk, xg, pb))
    d_tokens, s_q, s_k, s_v, s_out, s_up, s_down, sums = backward(
        dp, far, attended, lse, received, vectors, block_ids, xk, early,
        qkv, xg, pb, tokens, d_hidden, normed_t, padded,
    )
    slope = jax.nn.sigmoid(query_scale) / softplus
    if far:
        scale = jnp.pad(slope, (0, HP - HD))[None, :]
        final = list(
            finish(
                dp, cols, scale, sums, vectors,
                (output, d_tokens, s_q, s_k, s_v, s_out, s_up, s_down),
            )
        )
        final[6] = final[6][:HD]
        final[7], final[11] = final[7].T, final[11].T
        return tuple(final)
    else:
        dots = lax.psum(jnp.sum(s_q * padded.astype(F32), axis=(0, 2)), ("dp", "tensor"))
        sums = lax.psum(sums, ("dp", "tensor"))
        s_qkv = scatter_dp(jnp.concatenate([trim_heads(g) for g in s_q], axis=1), dp)
        s_q, s_k, s_v = (s_qkv[:, i * cols : (i + 1) * cols] for i in range(3))
        both = xk.astype(F32) + swap(xg, "tensor", tensor, 2).astype(F32)
        both = scatter_dp(both, dp)
        s_up, s_down = both[:, :cols], both[:, cols:].T
        both = scatter_dp(pb.astype(F32), dp)
        s_out = (both[:, :cols] + swap(both[:, cols:], "tensor", tensor, 2)).T
    d_scale = sums[6, :HD] * slope
    return (
        output,
        d_tokens,
        dots / attn_gain,
        s_q,
        s_k,
        s_v,
        d_scale,
        s_out,
        sums[0],
        s_up,
        sums[2:6, :cols].reshape(4 * cols),
        s_down,
        sums[1],
    )


def solution(mesh):
    weight, turned, whole = P("dp", "tensor"), P("tensor", "dp"), P()
    positions = P(("dp", "tensor"), None)
    return jax.shard_map(
        lambda *args: body(mesh.shape["dp"], mesh.shape["tensor"], *args),
        mesh=mesh,
        in_specs=(positions, positions, P("dp", None), whole, weight, weight, weight, whole,
                  turned, whole, weight, whole, turned, whole),
        out_specs=(positions, positions, whole, weight, weight, weight, whole, turned, whole,
                   weight, whole, turned, whole),
        check_vma=False,
    )
```

profile of v0, /device:TPU:0, one launch (start us, length us, event | category | flops | bytes accessed | tf_op | source)
XLA Modules:
  0.0 246.3 jit_solution(15610677320527715217)
XLA Ops:
  0.7 0.7 broadcast_multiply_fusion
  1.3 0.5 pad_bitcast_fusion.refs_0_
  1.8 0.9 fusion
  2.8 0.8 concatenate.3
  3.6 0.6 reshape.42.refs_1_.vec_ref.refs_3_.refs_2_
  4.2 99.9 %shard_map.237 = (bf16[3,2048,512]{2,1,0:T(8,128)(2,1)}, bf16[1280,2048]{1,0:T(8,128)(2,1)}, bf16[3,1280,512]{2,1,0:T(8,128)(2,1)}, bf16[4,80,2048]{2,1,0:T(8,12...) custom-call(bf16[512,1280]{1,0:T(8,128)(2,1)} %refs_10_.1, ...), custom_call_target="tpu_custom_call" | custom-call | tf_op jit(solution)/shard_map/pallas_call | solution.py:416
  104.1 34.8 %shard_map.238 = (bf16[512,1280]{1,0:T(8,128)(2,1)}, f32[512,1280]{1,0:T(8,128)}, bf16[2,4,128,640]{3,2,1,0:T(8,128)(2,1)}, bf16[1280,640]{1,0:T(8,128)(2,1)}, b...) custom-call(bf16[512,1280]{1,0:T(8,128)(2,1)} %refs_10_.1, bf16[512,1280]{1,0:T(8,128)(2,1)} %cot_ref.1, ...), custom_call_target="tpu_custom_call" | custom-call | tf_op jit(solution)/shard_map/pallas_call | solution.py:621
  138.9 102.2 %shard_map.239 = (bf16[512,1280]{1,0:T(8,128)(2,1)}, f32[160,320]{1,0:T(8,128)}, f32[160,320]{1,0:T(8,128)}, f32[160,320]{1,0:T(8,128)}, f32[160,320]{1,0:T(8,12...) custom-call(bf16[4,80,2048]{2,1,0:T(8,128)(2,1)} %get-tuple-element.49.refs_0_, ...), custom_call_target="tpu_custom_call" | custom-call | tf_op jit(solution)/shard_map/pallas_call | solution.py:1079
  241.2 4.9 %shard_map.240 = (bf16[512,1280]{1,0:T(8,128)(2,1)}, bf16[512,1280]{1,0:T(8,128)(2,1)}, f32[1280]{0:T(1024)}, f32[160,320]{1,0:T(8,128)}, f32[160,320]{1,0:T(8,1...) custom-call(f32[1,128]{1,0:T(1,128)} %pad_bitcast_fusion.refs_0_, ...), custom_call_target="tpu_custom_call" | custom-call | tf_op jit(solution)/shard_map/pallas_call | solution.py:1170
  (3 shorter events, 0.0 us)
where the time goes:
time: 247 us; the launch traced here: 246 us
  Pallas kernels  242 us (98%)
  local copies, waits for them, and re-layouts  2.84 us (1%)
    pallas_call x1, Pallas kernels, backward(): pl.pallas_call(lambda *refs: back_kernel(dp, far, *refs), out_shape=[jax....  102 us
    pallas_call x1, Pallas kernels, front(): pl.pallas_call(lambda *refs: front_kernel(dp, far, *refs), out_shape=[jax...  99.9 us
    pallas_call x1, Pallas kernels, middle(): pl.pallas_call(mid_kernel, out_shape=[jax.ShapeDtypeStruct((rows, width),...  34.8 us

commit v1 on v0

--- a/solution.py
+++ b/solution.py
@@ -660,8 +660,8 @@
     dtok_ref, dq_out, dk_out, dv_out, dout_ref, dup_ref, ddown_ref, sums_ref,
     do, dka, dva, kt_ref, idc_ref, dqkv, tok, dhid, normt, wpad,
     xrec, pbown, yrec, zrec, last, lastsend, lastrec,
-    gpay, gyrec, gzrec, ownsum, near, fo, crec, fs, frec, nrec, qsum, lvec, ar, arec, aorder,
-    so, sxa, rxa, sy, ry, sz, rz, sl, rl, sgy, rgy, sgz, rgz, sfo, rfo, sfs, rfs, sno, rno, sar, rar,
+    gpay, gyrec, gzrec, ownsum, near, fo, crec, fs, frec, nrec, qsum, lvec, ar, arec, aorder, er, erec, eorder,
+    so, sxa, rxa, sy, ry, sz, rz, sl, rl, sgy, rgy, sgz, rgz, sfo, rfo, sfs, rfs, sno, rno, sar, rar, ser, rer,
 ):
     here, me = lax.axis_index("tensor"), lax.axis_index("dp")
     heads, _, length = o_ref.shape
@@ -746,7 +746,41 @@
             z_send(p, step).wait_recv()
             last[p] += zrec[p, step - 1].astype(F32)
 
-    if fused:
+    def e_hop(n, where):
+        return remote(er.at[n], erec.at[n], ser.at[n], rer.at[n], where)
+
+    def e_last():
+        return remote(er.at[3], erec.at[2], ser.at[2], rer.at[2], at(2))
+
+    def e_z(step):
+        return remote(er.at[2], erec.at[3 + step], ser.at[3 + step], rer.at[3 + step], along(step))
+
+    def early_hop(h):
+        @pl.when(h == 0)
+        def _():
+            e_hop(0, at(1)).wait_recv()
+            er[1] = er[0] + erec[0]
+            e_hop(1, across).start()
+
+        @pl.when(h == 1)
+        def _():
+            e_hop(1, across).wait_recv()
+            er[2] = er[1] + erec[1]
+            for step in range(1, far):
+                e_z(step).start()
+
+        @pl.when(h == 2)
+        def _():
+            eorder[major] = er[2]
+            for step in range(1, far):
+                e_z(step).wait_recv()
+                eorder[lax.rem(major + far - step, far)] = erec[3 + step]
+            er[3] = (eorder[0] + eorder[1]) + (eorder[2] + eorder[3])
+            e_last().start()
+
+    if fused:
+        er[0] = early_ref[0:8, :]
+        e_hop(0, at(1)).start()
         for step in turn:
             x_send(step).start()
             y_send(1, step).start()
@@ -860,6 +894,7 @@
     def _(h):
         one_head(h)
         if fused:
+            early_hop(h)
             after_x(lax.rem(h + 1, far))
 
             @pl.when(h < 2)
@@ -868,21 +903,15 @@
                 def _(k):
                     after_y(1, lax.rem(2 * h + k + 1, far))
 
-            @pl.when(h > 0)
-            def _():
-                after_y(0, h)
-
             @pl.when(h == 1)
             def _():
                 for copy in loads[:2]:
                     copy.wait()
                 weight_pair(0)
 
-            @pl.when(h == 2)
+            @pl.when(h > 0)
             def _():
-                @pl.loop(0, far)
-                def _(j):
-                    gz_start(0, lax.rem(j + 1, far))
+                after_y(0, h)
 
     if not fused:
         for copy in loads[:2]:
@@ -922,12 +951,17 @@
         far_chunk(0)
         far_sum(0)
         x_far(0).start()
+
+        @pl.loop(0, far)
+        def _(j):
+            gz_start(0, lax.rem(j + 1, far))
+
         after_y(0, turn[far - 1])
         weight_pair(1)
-        ar[0] = jnp.zeros_like(ar[0])
-        ar[0, 0:6, :] = early_ref[0:6, :]
-        ar[0, 6:7, 0:HP] = qsum[0:1, :]
-        ar[0, 8:16, 0:depth] = lvec[0] + lvec[1]
+        for index in range(dp):
+            spot = slice(index * depth, (index + 1) * depth)
+            ar[0, :, spot] = lvec[0, index : index + 1, :] + lvec[1, index : index + 1, :]
+        ar[0, :, width:] = qsum[0:1, :]
         hop(0, at(1)).start()
         for c in range(1, count):
             far_chunk(c)
@@ -1026,7 +1060,12 @@
         for step in range(1, far):
             z_hop(step).wait_recv()
             aorder[lax.rem(major + far - step, far)] = arec[3 + step]
-        sums_ref[...] = (aorder[0] + aorder[1]) + (aorder[2] + aorder[3])
+        total = (aorder[0] + aorder[1]) + (aorder[2] + aorder[3])
+        e_last().wait_recv()
+        sums_ref[...] = jnp.zeros_like(sums_ref)
+        sums_ref[0:8, :] = er[3] + erec[2]
+        sums_ref[6:7, 0:HP] = total[:, width:]
+        sums_ref[7:8, :] = total[:, :width]
     else:
         dk_out[...] = jnp.zeros_like(dk_out)
         dv_out[...] = jnp.zeros_like(dv_out)
@@ -1047,12 +1086,16 @@
                 gz_send(0, step).wait_send()
                 gz_send(1, step).wait_send()
                 z_hop(step).wait_send()
+                e_z(step).wait_send()
                 for p in range(2):
                     z_send(p, step).wait_send()
         cross.wait_send()
         hop(0, at(1)).wait_send()
         hop(1, at(2)).wait_send()
         hop(2, across).wait_send()
+        e_hop(0, at(1)).wait_send()
+        e_hop(1, across).wait_send()
+        e_last().wait_send()
 
 
 def backward(dp, far, o, lse, drec, vectors, idr, xk, early, qkv, xg, pb,
@@ -1112,16 +1155,19 @@
             buf(count, TILE, width, only=False),
             buf(8, HP, dtype=F32, only=False),
             buf(2, dp, depth, dtype=F32),
-            buf(4, 16, width, dtype=F32),
-            buf(3 + far_n, 16, width, dtype=F32),
-            buf(far_n, 16, width, dtype=F32),
+            buf(4, 1, width + HP, dtype=F32),
+            buf(3 + far_n, 1, width + HP, dtype=F32),
+            buf(far_n, 1, width + HP, dtype=F32),
+            buf(4, 8, width, dtype=F32),
+            buf(3 + far_n, 8, width, dtype=F32),
+            buf(far_n, 8, width, dtype=F32),
             sem((6,)),
             sem((far_n,)), sem((far_n,)),
             sem((2, far_n)), sem((2, far_n)), sem((2, far_n)), sem((2, far_n)),
             sem, sem,
             sem((2, far_n)), sem((2, far_n)), sem((2, far_n)), sem((2, far_n)),
             sem((count,)), sem((count,)), sem((count,)), sem((count,)), sem((count,)), sem((count,)),
-            sem((3 + far_n,)), sem((3 + far_n,)),
+            sem((3 + far_n,)), sem((3 + far_n,)), sem((3 + far_n,)), sem((3 + far_n,)),
         ],
         compiler_params=pltpu.CompilerParams(
             vmem_limit_bytes=62 << 20, collective_id=3, has_side_effects=True
@@ -1134,7 +1180,6 @@
     moves, outs, held = refs[:8], refs[8:21], refs[21:29]
     row, sem = refs[29:]
     width = vec_ref.shape[1]
-    depth = width // dp
     places = (0, 1, 3, 4, 5, 7, 9, 11)
     enter = [pltpu.make_async_copy(moves[i], held[i], sem.at[i]) for i in range(8)]
     leave = [pltpu.make_async_copy(held[i], outs[places[i]], sem.at[8 + i]) for i in range(8)]
@@ -1146,9 +1191,7 @@
     row[...] = jnp.zeros_like(row)
     for i in range(width // cols):
         row[0:1, i * cols : (i + 1) * cols] = sums_ref[2 + i : 3 + i, :cols]
-    for i in range(dp):
-        spot = slice(i * depth, (i + 1) * depth)
-        row[1:2, spot] = sums_ref[8 + i : 9 + i, :depth] / vec_ref[0:1, spot]
+    row[1:2, :] = sums_ref[7:8, :] / vec_ref[0:1, :]
     outs[10][...] = row[0, :]
     outs[2][...] = row[1, :]
     for come, go in zip(enter, leave):

time: 247 us -> 243 us (0.984)
  Pallas kernels: 242 us -> 238 us
    pallas_call x1, Pallas kernels: 102 us -> 98.5 us  [backward(): pl.pallas_call(lambda *refs: back_kernel(dp, far, *refs), out_shape=[jax....]
where the time goes in v1:
time: 243 us
  Pallas kernels  238 us (98%)
  local copies, waits for them, and re-layouts  2.84 us (1%)
    pallas_call x1, Pallas kernels, front(): pl.pallas_call(lambda *refs: front_kernel(dp, far, *refs), out_shape=[jax...  99.9 us
    pallas_call x1, Pallas kernels, backward(): pl.pallas_call(lambda *refs: back_kernel(dp, far, *refs), out_shape=[jax....  98.5 us
    pallas_call x1, Pallas kernels, middle(): pl.pallas_call(mid_kernel, out_shape=[jax.ShapeDtypeStruct((rows, width),...  34.8 us
    pallas_call x1, Pallas kernels, finish(): pl.pallas_call(lambda *refs: finish_kernel(dp, cols, *refs), out_shape=sh...  4.93 us

profile of v1, /device:TPU:0, one launch (start us, length us, event | category | flops | bytes accessed | tf_op | source)
XLA Modules:
  0.0 242.5 jit_solution(10871728008764034288)
XLA Ops:
  0.7 0.7 broadcast_multiply_fusion
  1.3 0.5 pad_bitcast_fusion.refs_0_
  1.8 0.9 fusion
  2.8 0.8 concatenate.3
  3.6 0.6 reshape.42.refs_1_.vec_ref.refs_3_.refs_2_
  4.2 99.9 %shard_map.237 = (bf16[3,2048,512]{2,1,0:T(8,128)(2,1)}, bf16[1280,2048]{1,0:T(8,128)(2,1)}, bf16[3,1280,512]{2,1,0:T(8,128)(2,1)}, bf16[4,80,2048]{2,1,0:T(8,12...) custom-call(bf16[512,1280]{1,0:T(8,128)(2,1)} %refs_10_.1, ...), custom_call_target="tpu_custom_call" | custom-call | tf_op jit(solution)/shard_map/pallas_call | solution.py:416
  104.1 34.8 %shard_map.238 = (bf16[512,1280]{1,0:T(8,128)(2,1)}, f32[512,1280]{1,0:T(8,128)}, bf16[2,4,128,640]{3,2,1,0:T(8,128)(2,1)}, bf16[1280,640]{1,0:T(8,128)(2,1)}, b...) custom-call(bf16[512,1280]{1,0:T(8,128)(2,1)} %refs_10_.1, bf16[512,1280]{1,0:T(8,128)(2,1)} %cot_ref.1, ...), custom_call_target="tpu_custom_call" | custom-call | tf_op jit(solution)/shard_map/pallas_call | solution.py:621
  138.9 98.5 %shard_map.239 = (bf16[512,1280]{1,0:T(8,128)(2,1)}, f32[160,320]{1,0:T(8,128)}, f32[160,320]{1,0:T(8,128)}, f32[160,320]{1,0:T(8,128)}, f32[160,320]{1,0:T(8,12...) custom-call(bf16[4,80,2048]{2,1,0:T(8,128)(2,1)} %get-tuple-element.49.refs_0_, ...), custom_call_target="tpu_custom_call" | custom-call | tf_op jit(solution)/shard_map/pallas_call | solution.py:1122
  237.4 4.9 %shard_map.240 = (bf16[512,1280]{1,0:T(8,128)(2,1)}, bf16[512,1280]{1,0:T(8,128)(2,1)}, f32[1280]{0:T(1024)}, f32[160,320]{1,0:T(8,128)}, f32[160,320]{1,0:T(8,1...) custom-call(f32[1,128]{1,0:T(1,128)} %pad_bitcast_fusion.refs_0_, ...), custom_call_target="tpu_custom_call" | custom-call | tf_op jit(solution)/shard_map/pallas_call | solution.py:1213
  (3 shorter events, 0.0 us)

commit v2 on v1

--- a/solution.py
+++ b/solution.py
@@ -1176,7 +1176,7 @@
       tokens, d_hidden, normt, wpad)
 
 
-def finish_kernel(dp, cols, scale_ref, sums_ref, vec_ref, *refs):
+def finish_kernel(cols, sums_ref, vec_ref, *refs):
     moves, outs, held = refs[:8], refs[8:21], refs[21:29]
     row, sem = refs[29:]
     width = vec_ref.shape[1]
@@ -1185,7 +1185,7 @@
     leave = [pltpu.make_async_copy(held[i], outs[places[i]], sem.at[8 + i]) for i in range(8)]
     for copy in enter:
         copy.start()
-    outs[6][...] = sums_ref[6, 0:HP] * scale_ref[0, :]
+    outs[6][...] = sums_ref[6, 0:HP] * vec_ref[5, 0:HP]
     outs[8][...] = sums_ref[0, :]
     outs[12][...] = sums_ref[1, :]
     row[...] = jnp.zeros_like(row)
@@ -1201,7 +1201,7 @@
         copy.wait()
 
 
-def finish(dp, cols, scale, sums, vectors, moves):
+def finish(cols, sums, vectors, moves):
     width = vectors.shape[1]
     vmem = pl.BlockSpec(memory_space=pltpu.VMEM)
     hbm = pl.BlockSpec(memory_space=pl.ANY)
@@ -1211,14 +1211,14 @@
     shapes += [like[5], row, like[6], row, like[7], row]
     small = (2, 6, 8, 10, 12)
     return pl.pallas_call(
-        lambda *refs: finish_kernel(dp, cols, *refs),
+        lambda *refs: finish_kernel(cols, *refs),
         out_shape=shapes,
-        in_specs=[vmem] * 3 + [hbm] * 8,
+        in_specs=[vmem] * 2 + [hbm] * 8,
         out_specs=[vmem if i in small else hbm for i in range(13)],
         scratch_shapes=[pltpu.VMEM(v.shape, v.dtype) for v in moves]
         + [pltpu.VMEM((8, width), F32), pltpu.SemaphoreType.DMA((16,))],
         compiler_params=pltpu.CompilerParams(vmem_limit_bytes=60 << 20),
-    )(scale, sums, vectors, *moves)
+    )(sums, vectors, *moves)
 
 
 def swap(v, axis, size, mask):
@@ -1258,7 +1258,10 @@
     factor = jnp.pad(SCORE_BASE / math.sqrt(HD) * softplus, (0, HP - HD))
     b_rel = jnp.concatenate([lax.dynamic_slice(b_up, (at * cols,), (cols,)) for at in order])
     repeat = jnp.pad(jnp.tile(factor, heads), (0, width - heads * HP))
-    vectors = jnp.concatenate([attn_gain, mlp_gain, b_rel, b_down, repeat]).reshape(5, width)
+    slope = jax.nn.sigmoid(query_scale) / softplus
+    vectors = jnp.concatenate(
+        [attn_gain, mlp_gain, b_rel, b_down, repeat, jnp.pad(slope, (0, width - HD))]
+    ).reshape(6, width)
 
     far = dp // 2 if dp == 8 else 0
     matrices = (w_query, w_key, w_value, w_out.T, w_up, w_down.T)
@@ -1287,12 +1290,10 @@
         dp, far, attended, lse, received, vectors, block_ids, xk, early,
         qkv, xg, pb, tokens, d_hidden, normed_t, padded,
     )
-    slope = jax.nn.sigmoid(query_scale) / softplus
     if far:
-        scale = jnp.pad(slope, (0, HP - HD))[None, :]
         final = list(
             finish(
-                dp, cols, scale, sums, vectors,
+                cols, sums, vectors,
                 (output, d_tokens, s_q, s_k, s_v, s_out, s_up, s_down),
             )
         )

time: 243 us -> 243 us (level)
  no operation moved by 1% of the time
where the time goes in v2:
time: 243 us; the launch traced here: 242 us
  Pallas kernels  238 us (98%)
    pallas_call x1, Pallas kernels, front(): pl.pallas_call(lambda *refs: front_kernel(dp, far, *refs), out_shape=[jax...  99.9 us
    pallas_call x1, Pallas kernels, backward(): pl.pallas_call(lambda *refs: back_kernel(dp, far, *refs), out_shape=[jax....  98.5 us
    pallas_call x1, Pallas kernels, middle(): pl.pallas_call(mid_kernel, out_shape=[jax.ShapeDtypeStruct((rows, width),...  34.8 us
    pallas_call x1, Pallas kernels, finish(): pl.pallas_call(lambda *refs: finish_kernel(cols, *refs), out_shape=shapes...  4.93 us

profile of v2, /device:TPU:0, one launch (start us, length us, event | category | flops | bytes accessed | tf_op | source)
XLA Modules:
  0.0 242.1 jit_solution(7619309558064662194)
XLA Ops:
  0.7 0.7 multiply_divide_fusion
  1.4 0.9 fusion.1
  2.3 0.8 concatenate.3
  3.1 0.6 reshape.42.refs_1_.vec_ref.refs_3_
  3.7 99.9 %shard_map.237 = (bf16[3,2048,512]{2,1,0:T(8,128)(2,1)}, bf16[1280,2048]{1,0:T(8,128)(2,1)}, bf16[3,1280,512]{2,1,0:T(8,128)(2,1)}, bf16[4,80,2048]{2,1,0:T(8,12...) custom-call(bf16[512,1280]{1,0:T(8,128)(2,1)} %refs_10_.1, ...), custom_call_target="tpu_custom_call" | custom-call | tf_op jit(solution)/shard_map/pallas_call | solution.py:416
  103.6 34.8 %shard_map.238 = (bf16[512,1280]{1,0:T(8,128)(2,1)}, f32[512,1280]{1,0:T(8,128)}, bf16[2,4,128,640]{3,2,1,0:T(8,128)(2,1)}, bf16[1280,640]{1,0:T(8,128)(2,1)}, b...) custom-call(bf16[512,1280]{1,0:T(8,128)(2,1)} %refs_10_.1, bf16[512,1280]{1,0:T(8,128)(2,1)} %cot_ref.1, ...), custom_call_target="tpu_custom_call" | custom-call | tf_op jit(solution)/shard_map/pallas_call | solution.py:621
  138.4 98.5 %shard_map.239 = (bf16[512,1280]{1,0:T(8,128)(2,1)}, f32[160,320]{1,0:T(8,128)}, f32[160,320]{1,0:T(8,128)}, f32[160,320]{1,0:T(8,128)}, f32[160,320]{1,0:T(8,12...) custom-call(bf16[4,80,2048]{2,1,0:T(8,128)(2,1)} %get-tuple-element.49.refs_0_, ...), custom_call_target="tpu_custom_call" | custom-call | tf_op jit(solution)/shard_map/pallas_call | solution.py:1122
  236.9 4.9 %shard_map.240 = (bf16[512,1280]{1,0:T(8,128)(2,1)}, bf16[512,1280]{1,0:T(8,128)(2,1)}, f32[1280]{0:T(1024)}, f32[160,320]{1,0:T(8,128)}, f32[160,320]{1,0:T(8,1...) custom-call(f32[16,1280]{1,0:T(8,128)} %get-tuple-element.63.refs_0_, ...), custom_call_target="tpu_custom_call" | custom-call | tf_op jit(solution)/shard_map/pallas_call | solution.py:1213
  (4 shorter events, 0.0 us)

commit v3 on v2

--- a/solution.py
+++ b/solution.py
@@ -948,7 +948,8 @@
         return remote(ar.at[3], arec.at[3 + step], sar.at[3 + step], rar.at[3 + step], along(step))
 
     if fused:
-        far_chunk(0)
+        for c in range(count):
+            far_chunk(c)
         far_sum(0)
         x_far(0).start()
 
@@ -963,8 +964,6 @@
             ar[0, :, spot] = lvec[0, index : index + 1, :] + lvec[1, index : index + 1, :]
         ar[0, :, width:] = qsum[0:1, :]
         hop(0, at(1)).start()
-        for c in range(1, count):
-            far_chunk(c)
 
         @pl.loop(1, 3)
         def _(step):

time: 243 us -> 243 us (level)
  no operation moved by 1% of the time
where the time goes in v3:
time: 243 us; the launch traced here: 242 us
  Pallas kernels  239 us (98%)
    pallas_call x1, Pallas kernels, front(): pl.pallas_call(lambda *refs: front_kernel(dp, far, *refs), out_shape=[jax...  99.9 us
    pallas_call x1, Pallas kernels, backward(): pl.pallas_call(lambda *refs: back_kernel(dp, far, *refs), out_shape=[jax....  98.9 us
    pallas_call x1, Pallas kernels, middle(): pl.pallas_call(mid_kernel, out_shape=[jax.ShapeDtypeStruct((rows, width),...  34.8 us
    pallas_call x1, Pallas kernels, finish(): pl.pallas_call(lambda *refs: finish_kernel(cols, *refs), out_shape=shapes...  4.93 us

profile of v3, /device:TPU:0, one launch (start us, length us, event | category | flops | bytes accessed | tf_op | source)
XLA Modules:
  0.0 242.5 jit_solution(15368788995347920112)
XLA Ops:
  0.7 0.7 multiply_divide_fusion
  1.4 0.9 fusion.1
  2.3 0.8 concatenate.3
  3.1 0.6 reshape.42.refs_1_.vec_ref.refs_3_
  3.7 99.9 %shard_map.237 = (bf16[3,2048,512]{2,1,0:T(8,128)(2,1)}, bf16[1280,2048]{1,0:T(8,128)(2,1)}, bf16[3,1280,512]{2,1,0:T(8,128)(2,1)}, bf16[4,80,2048]{2,1,0:T(8,12...) custom-call(bf16[512,1280]{1,0:T(8,128)(2,1)} %refs_10_.1, ...), custom_call_target="tpu_custom_call" | custom-call | tf_op jit(solution)/shard_map/pallas_call | solution.py:416
  103.6 34.8 %shard_map.238 = (bf16[512,1280]{1,0:T(8,128)(2,1)}, f32[512,1280]{1,0:T(8,128)}, bf16[2,4,128,640]{3,2,1,0:T(8,128)(2,1)}, bf16[1280,640]{1,0:T(8,128)(2,1)}, b...) custom-call(bf16[512,1280]{1,0:T(8,128)(2,1)} %refs_10_.1, bf16[512,1280]{1,0:T(8,128)(2,1)} %cot_ref.1, ...), custom_call_target="tpu_custom_call" | custom-call | tf_op jit(solution)/shard_map/pallas_call | solution.py:621
  138.4 98.9 %shard_map.239 = (bf16[512,1280]{1,0:T(8,128)(2,1)}, f32[160,320]{1,0:T(8,128)}, f32[160,320]{1,0:T(8,128)}, f32[160,320]{1,0:T(8,128)}, f32[160,320]{1,0:T(8,12...) custom-call(bf16[4,80,2048]{2,1,0:T(8,128)(2,1)} %get-tuple-element.49.refs_0_, ...), custom_call_target="tpu_custom_call" | custom-call | tf_op jit(solution)/shard_map/pallas_call | solution.py:1121
  237.3 4.9 %shard_map.240 = (bf16[512,1280]{1,0:T(8,128)(2,1)}, bf16[512,1280]{1,0:T(8,128)(2,1)}, f32[1280]{0:T(1024)}, f32[160,320]{1,0:T(8,128)}, f32[160,320]{1,0:T(8,1...) custom-call(f32[16,1280]{1,0:T(8,128)} %get-tuple-element.63.refs_0_, ...), custom_call_target="tpu_custom_call" | custom-call | tf_op jit(solution)/shard_map/pallas_call | solution.py:1212
  (4 shorter events, 0.0 us)
